TPU v7x, 32 devices: a whole 2x2x4 slice. The times are simulated.
32 devices in a mesh: fsdp: 2 (over y), ctx: 4 (over z), tp: 4 (over x, core).
Axes of the slice: x: 2, y: 2, z: 4, core: 2. Of those that a mesh axis runs over, the one named last changes fastest.
Arguments:
- tokens: bfloat16 [4, 4, 1024, 1024], P(None, 'fsdp', 'ctx', 'tp'), may hold values from -6 to 6
- skip_tokens: bfloat16 [4, 4, 1024, 1024], P(None, 'fsdp', 'ctx', 'tp'), may hold values from -6 to 6
- merger_weight: bfloat16 [1024, 2, 1024], P(('fsdp', 'ctx'), None, 'tp'), may hold values from -0.125 to 0.125
- merger_bias: float32 [1024], P(('fsdp', 'ctx', 'tp')), may hold values from -3 to 3
- first_gain: float32 [1024], P(('fsdp', 'ctx', 'tp')), may hold values from 0.25 to 1.75
- first_shift: float32 [1024], P(('fsdp', 'ctx', 'tp')), may hold values from -2 to 2
- attend_weight: bfloat16 [1024, 3, 1024], P(('fsdp', 'ctx'), None, 'tp'), may hold values from -0.25 to 0.25
- output_weight: bfloat16 [1024, 1024], P(('fsdp', 'ctx'), 'tp'), may hold values from -0.75 to 0.75
- output_bias: float32 [1024], P(('fsdp', 'ctx', 'tp')), may hold values from -2 to 2
- second_gain: float32 [1024], P(('fsdp', 'ctx', 'tp')), may hold values from 0.25 to 1.75
- second_shift: float32 [1024], P(('fsdp', 'ctx', 'tp')), may hold values from -2 to 2
- expand_weight: bfloat16 [1024, 4096], P(('fsdp', 'ctx'), 'tp'), may hold values from -0.1875 to 0.1875
- widen_bias: float32 [4096], P(('fsdp', 'ctx', 'tp')), may hold values from -3 to 3
- shrink_weight: bfloat16 [1024, 4096], P(('fsdp', 'ctx'), 'tp'), may hold values from -0.125 to 0.125
- shrink_bias: float32 [1024], P(('fsdp', 'ctx', 'tp')), may hold values from -2 to 2
- live_slots: int32 [4, 4], P(None, 'fsdp'), may hold values from 0 to 1, as said below
- cotangent: bfloat16 [4, 4, 1024, 1024], P(None, 'fsdp', ('ctx', 'tp')), may hold values from -6 to 6
Outputs:
- layer_out: bfloat16 [4, 4, 1024, 1024], P(None, 'fsdp', ('ctx', 'tp'))
- grad_tokens: float32 [4, 4, 1024, 1024], P(None, 'fsdp', 'ctx', 'tp')
- grad_skip: float32 [4, 4, 1024, 1024], P(None, 'fsdp', 'ctx', 'tp')
- weight_merger: float32 [1024, 2, 1024], P(('fsdp', 'ctx'), None, 'tp')
- bias_merger: float32 [1024], P(('fsdp', 'ctx', 'tp'))
- gain_first: float32 [1024], P(('fsdp', 'ctx', 'tp'))
- shift_first: float32 [1024], P(('fsdp', 'ctx', 'tp'))
- weight_attend: float32 [1024, 3, 1024], P(('fsdp', 'ctx'), None, 'tp')
- weight_output: float32 [1024, 1024], P(('fsdp', 'ctx'), 'tp')
- bias_output: float32 [1024], P(('fsdp', 'ctx', 'tp'))
- gain_second: float32 [1024], P(('fsdp', 'ctx', 'tp'))
- shift_second: float32 [1024], P(('fsdp', 'ctx', 'tp'))
- weight_expand: float32 [1024, 4096], P(('fsdp', 'ctx'), 'tp')
- bias_expand: float32 [4096], P(('fsdp', 'ctx', 'tp'))
- weight_shrink: float32 [1024, 4096], P(('fsdp', 'ctx'), 'tp')
- bias_shrink: float32 [1024], P(('fsdp', 'ctx', 'tp'))
Inputs may be any that keep to these rules, and one draw needn't show every extreme that they name: `live_slots`: in every micro-batch but the last exactly one of the 4 slots is empty (0), in the last exactly two; the empty slots lie anywhere.
All inputs are finite; a program needn't handle non-finite values.
Results may differ from a plain program's by a relative error of at most 0.017.
Values may be sent and summed in bfloat16 or wider, within the bound.
No kernel may reach another device: no remote copies, remote signals or barrier semaphores. Data moves between devices by JAX's collectives and lax.ppermute only.
A program may use at most 256 MiB of HBM per device.

v0:
```python
import jax
import jax.numpy as jnp
from jax import lax
from jax.sharding import PartitionSpec as P

HD = 64
EPSILON = 1e-05


def layer_norm(matrix, scales, shifts):
    center = matrix - jnp.mean(matrix, axis=-1, keepdims=True)
    spread = jnp.mean(center * center, axis=-1, keepdims=True)
    return center * lax.rsqrt(spread + EPSILON) * scales + shifts


def gelu_exact(matrix):
    return jax.nn.gelu(matrix, approximate=False)


def fetch(merger_part, attend_part, output_part, expand_part, shrink_part):
    return (
        lax.all_gather(merger_part, ("fsdp", "ctx"), axis=0, tiled=True),
        lax.all_gather(attend_part, ("fsdp", "ctx"), axis=0, tiled=True),
        lax.all_gather(output_part, ("fsdp", "ctx"), axis=0, tiled=True),
        lax.all_gather(expand_part, ("fsdp", "ctx"), axis=0, tiled=True),
        lax.all_gather(shrink_part, ("fsdp", "ctx"), axis=0, tiled=True),
    )


def spread_rows(block):
    return lax.all_gather(block, "tp", axis=1, tiled=True)


def fold_rows(block):
    return lax.psum_scatter(block, "tp", scatter_dimension=1, tiled=True)


def reduce_weights(parts):
    return (
        lax.psum_scatter(parts[0], ("fsdp", "ctx"), scatter_dimension=0, tiled=True),
        lax.psum_scatter(parts[1], ("fsdp", "ctx"), scatter_dimension=0, tiled=True),
        lax.psum_scatter(parts[2], ("fsdp", "ctx"), scatter_dimension=0, tiled=True),
        lax.psum_scatter(parts[3], ("fsdp", "ctx"), scatter_dimension=0, tiled=True),
        lax.psum_scatter(parts[4], ("fsdp", "ctx"), scatter_dimension=0, tiled=True),
    )


def micro_step(weights, vectors, tokens_now, skips_now, live_now, cot_now, tensor_rank):
    merger_full, attend_full, output_full, expand_full, shrink_full = weights
    (
        merger_bias,
        first_gain,
        first_shift,
        output_bias,
        second_gain,
        second_shift,
        shrink_bias,
        widen_bias,
    ) = vectors
    groups = tokens_now.shape[0]
    local_len = tokens_now.shape[1]
    heads_dev = attend_full.shape[2] // HD
    hidden = expand_full.shape[1]
    scaling = HD ** (-0.5)
    stacked = jnp.stack([tokens_now, skips_now], axis=2)
    joined = (
        fold_rows(
            jnp.einsum("stci,oci->sto", stacked, merger_full, preferred_element_type=jnp.float32)
        )
        + merger_bias
    )
    normed, first_pull = jax.vjp(layer_norm, joined, first_gain, first_shift)
    normed_all = spread_rows(normed.astype(jnp.bfloat16))
    project = jnp.einsum(
        "std,dcj->stcj", normed_all, attend_full, preferred_element_type=jnp.float32
    ).astype(jnp.bfloat16)
    key_rows, value_rows = (
        lax.all_gather(project[:, :, 1], "ctx", axis=1, tiled=True),
        lax.all_gather(project[:, :, 2], "ctx", axis=1, tiled=True),
    )
    seq_len = key_rows.shape[1]
    query_heads = project[:, :, 0].reshape(groups, local_len, heads_dev, HD)
    key_heads = key_rows.reshape(groups, seq_len, heads_dev, HD)
    value_heads = value_rows.reshape(groups, seq_len, heads_dev, HD)
    scores = (
        jnp.einsum("sqhd,skhd->shqk", query_heads, key_heads, preferred_element_type=jnp.float32)
        * scaling
    )
    row_peak = jnp.max(scores, axis=-1, keepdims=True)
    logsum = row_peak + jnp.log(jnp.sum(jnp.exp(scores - row_peak), axis=-1, keepdims=True))
    probs_low = jnp.exp(scores - logsum).astype(jnp.bfloat16)
    attended = jnp.einsum(
        "shqk,skhd->sqhd", probs_low, value_heads, preferred_element_type=jnp.float32
    )
    attended = attended.astype(jnp.bfloat16).reshape(groups, local_len, heads_dev * HD)
    second = (
        joined
        + fold_rows(
            jnp.einsum("sti,oi->sto", attended, output_full, preferred_element_type=jnp.float32)
        )
        + output_bias
    )
    normed_two, second_pull = jax.vjp(layer_norm, second, second_gain, second_shift)
    normed_two_all = spread_rows(normed_two.astype(jnp.bfloat16))
    bias_slice = lax.dynamic_slice_in_dim(widen_bias, tensor_rank * hidden, hidden)
    widened_hidden = (
        jnp.einsum("std,df->stf", normed_two_all, expand_full, preferred_element_type=jnp.float32)
        + bias_slice
    )
    activated, gelu_pull = jax.vjp(gelu_exact, widened_hidden)
    activated_low = activated.astype(jnp.bfloat16)
    result = (
        second
        + fold_rows(
            jnp.einsum(
                "stf,of->sto", activated_low, shrink_full, preferred_element_type=jnp.float32
            )
        )
        + shrink_bias
    )
    live_mask = live_now.astype(jnp.float32)[:, None, None]
    layer_out = (result * live_mask).astype(jnp.bfloat16)
    upstream = cot_now.astype(jnp.float32) * live_mask
    grad_shrink_bias = jnp.sum(upstream, axis=(0, 1))
    branch_low = spread_rows(upstream.astype(jnp.bfloat16))
    grad_shrink = jnp.einsum(
        "sto,stf->of", branch_low, activated_low, preferred_element_type=jnp.float32
    )
    grad_activated = jnp.einsum(
        "sto,of->stf", branch_low, shrink_full, preferred_element_type=jnp.float32
    )
    grad_expanded = gelu_pull(grad_activated)[0].astype(jnp.bfloat16)
    grad_expand_bias = jnp.sum(grad_expanded, axis=(0, 1), dtype=jnp.float32)
    grad_expand = jnp.einsum(
        "std,stf->df", normed_two_all, grad_expanded, preferred_element_type=jnp.float32
    )
    grad_normed_two = fold_rows(
        jnp.einsum("stf,df->std", grad_expanded, expand_full, preferred_element_type=jnp.float32)
    )
    grad_second_norm, grad_second_gain, grad_second_shift = second_pull(grad_normed_two)
    grad_second = upstream + grad_second_norm
    grad_output_bias = jnp.sum(grad_second, axis=(0, 1))
    attn_low = spread_rows(grad_second.astype(jnp.bfloat16))
    grad_output = jnp.einsum("sto,sti->oi", attn_low, attended, preferred_element_type=jnp.float32)
    grad_attended = jnp.einsum(
        "sto,oi->sti", attn_low, output_full, preferred_element_type=jnp.float32
    )
    grad_attended = grad_attended.astype(jnp.bfloat16).reshape(groups, local_len, heads_dev, HD)
    scores_again = (
        jnp.einsum("sqhd,skhd->shqk", query_heads, key_heads, preferred_element_type=jnp.float32)
        * scaling
    )
    probs = jnp.exp(scores_again - logsum)
    grad_probs = jnp.einsum(
        "sqhd,skhd->shqk", grad_attended, value_heads, preferred_element_type=jnp.float32
    )
    row_inner = jnp.sum(probs * grad_probs, axis=-1, keepdims=True)
    grad_scores = (probs * (grad_probs - row_inner)).astype(jnp.bfloat16)
    grad_queries = (
        jnp.einsum("shqk,skhd->sqhd", grad_scores, key_heads, preferred_element_type=jnp.float32)
        * scaling
    )
    probs_again = probs.astype(jnp.bfloat16)
    key_terms = (
        jnp.einsum("shqk,sqhd->skhd", grad_scores, query_heads, preferred_element_type=jnp.float32)
        * scaling
    )
    value_terms = jnp.einsum(
        "shqk,sqhd->skhd", probs_again, grad_attended, preferred_element_type=jnp.float32
    )
    grad_keys, grad_values = (
        lax.psum_scatter(
            key_terms.reshape(groups, seq_len, heads_dev * HD).astype(jnp.bfloat16),
            "ctx",
            scatter_dimension=1,
            tiled=True,
        ).astype(jnp.float32),
        lax.psum_scatter(
            value_terms.reshape(groups, seq_len, heads_dev * HD).astype(jnp.bfloat16),
            "ctx",
            scatter_dimension=1,
            tiled=True,
        ).astype(jnp.float32),
    )
    grad_project = jnp.stack(
        [
            grad_queries.reshape(groups, local_len, heads_dev * HD).astype(jnp.bfloat16),
            grad_keys.astype(jnp.bfloat16),
            grad_values.astype(jnp.bfloat16),
        ],
        axis=2,
    )
    grad_attend = jnp.einsum(
        "std,stcj->dcj", normed_all, grad_project, preferred_element_type=jnp.float32
    )
    grad_normed = fold_rows(
        jnp.einsum("stcj,dcj->std", grad_project, attend_full, preferred_element_type=jnp.float32)
    )
    grad_first_norm, gradient_leading_gain, grad_first_shift = first_pull(grad_normed)
    grad_joined = grad_second + grad_first_norm
    grad_merger_bias = jnp.sum(grad_joined, axis=(0, 1))
    joined_low = spread_rows(grad_joined.astype(jnp.bfloat16))
    grad_merger = jnp.einsum(
        "sto,stci->oci", joined_low, stacked, preferred_element_type=jnp.float32
    )
    grad_stacked = jnp.einsum(
        "sto,oci->stci", joined_low, merger_full, preferred_element_type=jnp.float32
    )
    expand_whole = lax.dynamic_update_slice_in_dim(
        jnp.zeros((widen_bias.shape[0],), jnp.float32), grad_expand_bias, tensor_rank * hidden, 0
    )
    weight_part = (grad_merger, grad_attend, grad_output, grad_expand, grad_shrink)
    vector_portion = (
        grad_merger_bias,
        gradient_leading_gain,
        grad_first_shift,
        grad_output_bias,
        grad_second_gain,
        grad_second_shift,
        grad_shrink_bias,
        expand_whole,
    )
    return (layer_out, grad_stacked[:, :, 0], grad_stacked[:, :, 1], weight_part, vector_portion)


def on_device(
    tokens,
    skip_tokens,
    merger_weight,
    merger_bias,
    first_gain,
    first_shift,
    attend_weight,
    output_weight,
    output_bias,
    second_gain,
    second_shift,
    expand_weight,
    widen_bias,
    shrink_weight,
    shrink_bias,
    live_slots,
    cotangent,
):
    tensor_rank = lax.axis_index("tp")
    vectors = (
        lax.all_gather(merger_bias, ("fsdp", "ctx", "tp"), axis=0, tiled=True),
        lax.all_gather(first_gain, ("fsdp", "ctx", "tp"), axis=0, tiled=True),
        lax.all_gather(first_shift, ("fsdp", "ctx", "tp"), axis=0, tiled=True),
        lax.all_gather(output_bias, ("fsdp", "ctx", "tp"), axis=0, tiled=True),
        lax.all_gather(second_gain, ("fsdp", "ctx", "tp"), axis=0, tiled=True),
        lax.all_gather(second_shift, ("fsdp", "ctx", "tp"), axis=0, tiled=True),
        lax.all_gather(shrink_bias, ("fsdp", "ctx", "tp"), axis=0, tiled=True),
        lax.all_gather(widen_bias, ("fsdp", "ctx", "tp"), axis=0, tiled=True),
    )
    batches = tokens.shape[0]
    outs_list = []
    token_list = []
    skip_list = []
    weight_totals = None
    vector_totals = None
    for batch_index in range(batches):
        current = fetch(merger_weight, attend_weight, output_weight, expand_weight, shrink_weight)
        layer_out, grad_one, gradient_remaining, weight_part, vector_portion = micro_step(
            current,
            vectors,
            tokens[batch_index],
            skip_tokens[batch_index],
            live_slots[batch_index],
            cotangent[batch_index],
            tensor_rank,
        )
        if weight_totals is None:
            weight_totals = weight_part
            vector_totals = vector_portion
        else:
            weight_totals = tuple(
                (former + latter for former, latter in zip(weight_totals, weight_part))
            )
            vector_totals = tuple(
                (former + latter for former, latter in zip(vector_totals, vector_portion))
            )
        outs_list.append(layer_out)
        token_list.append(grad_one)
        skip_list.append(gradient_remaining)
    weight_totals = reduce_weights(weight_totals)
    vector_grads = (
        lax.psum_scatter(vector_totals[0], ("fsdp", "ctx", "tp"), scatter_dimension=0, tiled=True),
        lax.psum_scatter(vector_totals[1], ("fsdp", "ctx", "tp"), scatter_dimension=0, tiled=True),
        lax.psum_scatter(vector_totals[2], ("fsdp", "ctx", "tp"), scatter_dimension=0, tiled=True),
        lax.psum_scatter(vector_totals[3], ("fsdp", "ctx", "tp"), scatter_dimension=0, tiled=True),
        lax.psum_scatter(vector_totals[4], ("fsdp", "ctx", "tp"), scatter_dimension=0, tiled=True),
        lax.psum_scatter(vector_totals[5], ("fsdp", "ctx", "tp"), scatter_dimension=0, tiled=True),
        lax.psum_scatter(vector_totals[6], ("fsdp", "ctx", "tp"), scatter_dimension=0, tiled=True),
        lax.psum_scatter(vector_totals[7], ("fsdp", "ctx", "tp"), scatter_dimension=0, tiled=True),
    )
    return (
        jnp.stack(outs_list, axis=0),
        jnp.stack(token_list, axis=0),
        jnp.stack(skip_list, axis=0),
        weight_totals[0],
        vector_grads[0],
        vector_grads[1],
        vector_grads[2],
        weight_totals[1],
        weight_totals[2],
        vector_grads[3],
        vector_grads[4],
        vector_grads[5],
        weight_totals[3],
        vector_grads[7],
        weight_totals[4],
        vector_grads[6],
    )


def solution(mesh):
    placed = (
        P(None, "fsdp", "ctx", "tp"),
        P(None, "fsdp", "ctx", "tp"),
        P(("fsdp", "ctx"), None, "tp"),
        P(("fsdp", "ctx", "tp")),
        P(("fsdp", "ctx", "tp")),
        P(("fsdp", "ctx", "tp")),
        P(("fsdp", "ctx"), None, "tp"),
        P(("fsdp", "ctx"), "tp"),
        P(("fsdp", "ctx", "tp")),
        P(("fsdp", "ctx", "tp")),
        P(("fsdp", "ctx", "tp")),
        P(("fsdp", "ctx"), "tp"),
        P(("fsdp", "ctx", "tp")),
        P(("fsdp", "ctx"), "tp"),
        P(("fsdp", "ctx", "tp")),
        P(None, "fsdp"),
        P(None, "fsdp", ("ctx", "tp"), None),
    )
    return jax.shard_map(
        on_device,
        mesh=mesh,
        in_specs=placed,
        out_specs=(
            P(None, "fsdp", ("ctx", "tp"), None),
            P(None, "fsdp", "ctx", "tp"),
            P(None, "fsdp", "ctx", "tp"),
            P(("fsdp", "ctx"), None, "tp"),
            P(("fsdp", "ctx", "tp")),
            P(("fsdp", "ctx", "tp")),
            P(("fsdp", "ctx", "tp")),
            P(("fsdp", "ctx"), None, "tp"),
            P(("fsdp", "ctx"), "tp"),
            P(("fsdp", "ctx", "tp")),
            P(("fsdp", "ctx", "tp")),
            P(("fsdp", "ctx", "tp")),
            P(("fsdp", "ctx"), "tp"),
            P(("fsdp", "ctx", "tp")),
            P(("fsdp", "ctx"), "tp"),
            P(("fsdp", "ctx", "tp")),
        ),
        check_vma=False,
    )
```

profile of v0, /device:TPU:0, one launch (start us, length us, event | category | flops | bytes accessed | tf_op | source)
XLA Modules:
  0.0 2147.7 jit_solution(7706245499468301437)
XLA Ops:
  10.6 43.0 %all-gather.42.cloned.1.call-done = bf16[1024,2,256]{2,0,1:T(8,128)(2,1)} async-done(((bf16[128,2,256]{2,0,1:T(8,128)(2,1)}), bf16[1024,2,256]{2,0,1:T(8,128)(2,1)}) %all-gather.42.cloned.1.call-update) | async-done | bytes 1048592 | tf_op jit(solution)/shard_map/all_gather | solution.py:22
  66.0 38.9 %all-reduce.16 = (f32[1024]{0:T(1024)S(1)}, f32[1024]{0:T(1024)S(1)}, f32[1024]{0:T(1024)S(1)}, f32[1024]{0:T(1024)S(1)}, f32[1024]{0:T(1024)S(1)}, /*index=5*/f32[1024]{0:T(1024)S(1)}) all-reduce(f32[1024]{0:T(1024)S(1)} %dynamic-update-slice.3, ...), channel_id=1, replica_groups=mesh['fsdp'=2,'ctx'=4,'tp'=4] {'fsdp','ctx','tp'}, use_global_device_ids=true, to_apply=%add | all-reduce | flops 6144 | bytes 49152
  106.2 16.1 reduce-scatter.40.cloned.1.call-done
  122.3 33.8 %reduce-scatter.46.cloned.1.call-done = f32[2,64,1024]{2,1,0:T(8,128)} async-done(((f32[2,256,1024]{2,1,0:T(8,128)}), f32[2,64,1024]{2,1,0:T(8,128)}) %reduce-scatter.46.cloned.1.call-update) | async-done | bytes 524304 | tf_op jit(solution)/shard_map/reduce_scatter | solution.py:35
  156.1 34.0 %reduce-scatter.52.cloned.1.call-done = f32[2,64,1024]{2,1,0:T(8,128)} async-done(((f32[2,256,1024]{2,1,0:T(8,128)}), f32[2,64,1024]{2,1,0:T(8,128)}) %reduce-scatter.52.cloned.1.call-update) | async-done | bytes 524304 | tf_op jit(solution)/shard_map/reduce_scatter | solution.py:35
  196.6 41.2 %all-gather.46.cloned.1.call-done = bf16[1024,3,256]{0,2,1:T(8,128)(2,1)} async-done(((bf16[128,3,256]{0,2,1:T(8,128)(2,1)}), bf16[1024,3,256]{0,2,1:T(8,128)(2,1)}) %all-gather.46.cloned.1.call-update) | async-done | bytes 1572880 | tf_op jit(solution)/shard_map/all_gather | solution.py:23
  237.9 17.1 all-gather.54.cloned.1.call-done
  259.2 14.7 all-gather.58.cloned.1.call-done
  278.1 14.7 all-gather.62.cloned.1.call-done
  297.0 14.5 all-gather.44.cloned.1.call-done
  315.2 34.9 %all_gather.146 = bf16[1024,256]{1,0:T(8,128)(2,1)S(1)} all-gather(bf16[128,256]{1,0:T(8,128)(2,1)S(1)} %copy-done.113), channel_id=1, replica_groups=mesh['fsdp'=2,'ctx'=4,'tp'=4] {'fsdp','ctx'}, dimensions={0}, use_global_device_ids=true | all-gather | bytes 589824 | tf_op jit(solution)/shard_map/all_gather | solution.py:24
  356.6 24.6 %all-gather.94.cloned.1.call-done = bf16[2,1024,1,256]{1,3,2,0:T(8,128)(2,1)} async-done(((bf16[2,256,1,256]{1,3,2,0:T(8,128)(2,1)}), bf16[2,1024,1,256]{1,3,2,0:T(8,128)(2,1)}) %all-gather.94.cloned.1.call-update) | async-done | bytes 1048592 | tf_op jit(solution)/shard_map/all_gather | solution.py:79
  388.5 23.4 %all-gather.100.cloned.1.call-done = bf16[2,1024,1,256]{1,3,2,0:T(8,128)(2,1)} async-done(((bf16[2,256,1,256]{1,3,2,0:T(8,128)(2,1)}), bf16[2,1024,1,256]{1,3,2,0:T(8,128)(2,1)}) %all-gather.100.cloned.1.call-update) | async-done | bytes 1048592 | tf_op jit(solution)/shard_map/all_gather | solution.py:78
  417.8 24.6 %all-gather.98.cloned.1.call-done = bf16[2,1024,1,256]{1,3,2,0:T(8,128)(2,1)} async-done(((bf16[2,256,1,256]{1,3,2,0:T(8,128)(2,1)}), bf16[2,1024,1,256]{1,3,2,0:T(8,128)(2,1)}) %all-gather.98.cloned.1.call-update) | async-done | bytes 1048592 | tf_op jit(solution)/shard_map/all_gather | solution.py:79
  449.9 23.1 %all-gather.104.cloned.1.call-done = bf16[2,1024,1,256]{1,3,2,0:T(8,128)(2,1)} async-done(((bf16[2,256,1,256]{1,3,2,0:T(8,128)(2,1)}), bf16[2,1024,1,256]{1,3,2,0:T(8,128)(2,1)}) %all-gather.104.cloned.1.call-update) | async-done | bytes 1048592 | tf_op jit(solution)/shard_map/all_gather | solution.py:78
  478.8 24.1 %all-gather.102.cloned.1.call-done = bf16[2,1024,1,256]{1,3,2,0:T(8,128)(2,1)} async-done(((bf16[2,256,1,256]{1,3,2,0:T(8,128)(2,1)}), bf16[2,1024,1,256]{1,3,2,0:T(8,128)(2,1)}) %all-gather.102.cloned.1.call-update) | async-done | bytes 1048592 | tf_op jit(solution)/shard_map/all_gather | solution.py:79
  510.2 23.3 %all-gather.92.cloned.1.call-done = bf16[2,1024,1,256]{1,3,2,0:T(8,128)(2,1)} async-done(((bf16[2,256,1,256]{1,3,2,0:T(8,128)(2,1)}), bf16[2,1024,1,256]{1,3,2,0:T(8,128)(2,1)}) %all-gather.92.cloned.1.call-update) | async-done | bytes 1048592 | tf_op jit(solution)/shard_map/all_gather | solution.py:78
  539.4 24.0 %all-gather.90.cloned.1.call-done = bf16[2,1024,1,256]{1,3,2,0:T(8,128)(2,1)} async-done(((bf16[2,256,1,256]{1,3,2,0:T(8,128)(2,1)}), bf16[2,1024,1,256]{1,3,2,0:T(8,128)(2,1)}) %all-gather.90.cloned.1.call-update) | async-done | bytes 1048592 | tf_op jit(solution)/shard_map/all_gather | solution.py:79
  571.4 24.9 %reduce-scatter.42.cloned.1.call-done = f32[2,64,1024]{2,1,0:T(8,128)} async-done(((f32[2,256,1024]{2,1,0:T(8,128)}), f32[2,64,1024]{2,1,0:T(8,128)}) %reduce-scatter.42.cloned.1.call-update) | async-done | bytes 524304 | tf_op jit(solution)/shard_map/reduce_scatter | solution.py:35
  596.2 34.6 %reduce-scatter.48.cloned.1.call-done = f32[2,64,1024]{2,1,0:T(8,128)} async-done(((f32[2,256,1024]{2,1,0:T(8,128)}), f32[2,64,1024]{2,1,0:T(8,128)}) %reduce-scatter.48.cloned.1.call-update) | async-done | bytes 524304 | tf_op jit(solution)/shard_map/reduce_scatter | solution.py:35
  630.8 34.0 %reduce-scatter.54.cloned.1.call-done = f32[2,64,1024]{2,1,0:T(8,128)} async-done(((f32[2,256,1024]{2,1,0:T(8,128)}), f32[2,64,1024]{2,1,0:T(8,128)}) %reduce-scatter.54.cloned.1.call-update) | async-done | bytes 524304 | tf_op jit(solution)/shard_map/reduce_scatter | solution.py:35
  664.8 34.2 %reduce-scatter.36.cloned.1.call-done = f32[2,64,1024]{2,1,0:T(8,128)} async-done(((f32[2,256,1024]{2,1,0:T(8,128)}), f32[2,64,1024]{2,1,0:T(8,128)}) %reduce-scatter.36.cloned.1.call-update) | async-done | bytes 524304 | tf_op jit(solution)/shard_map/reduce_scatter | solution.py:35
  711.8 41.1 %all-gather.8 = f32[32,1,128]{2,1,0:T(1,128)S(1)} all-gather(f32[1,1,128]{2,1,0:T(1,128)S(1)} %bitcast.612), channel_id=1, replica_groups=mesh['fsdp'=2,'ctx'=4,'tp'=4] {'fsdp','ctx','tp'}, dimensions={0}, use_global_device_ids=true | all-gather | bytes 16896 | tf_op jit(solution)/shard_map/all_gather | solution.py:254
  752.9 14.8 all-gather.60.cloned.1.call-done
  772.2 14.4 all-gather.64.cloned.1.call-done
  791.1 14.3 all-gather.56.cloned.1.call-done
  809.9 14.2 all-gather.48.cloned.1.call-done
  824.1 8.2 fusion.169
  833.6 21.4 multiply_convert_fusion.9
  855.1 38.8 %all-gather.52.cloned.1.call-done = bf16[1024,1024]{1,0:T(8,128)(2,1)} async-done(((bf16[128,1024]{1,0:T(8,128)(2,1)}), bf16[1024,1024]{1,0:T(8,128)(2,1)}) %all-gather.52.cloned.1.call-update) | async-done | bytes 2097168 | tf_op jit(solution)/shard_map/all_gather | solution.py:26
  893.9 5.8 convert_reduce_fusion
  903.4 7.2 all-gather.78.cloned.1.call-done
  910.6 5.8 convert_reduce_fusion.1
  920.0 8.9 all-gather.72.cloned.1.call-done
  928.9 5.8 convert_reduce_fusion.2
  938.6 8.7 all-gather.66.cloned.1.call-done
  947.2 5.8 convert_reduce_fusion.3
  956.7 24.9 %reduce-scatter.82.cloned.1.call-done = f32[2,64,1024]{2,1,0:T(8,128)} async-done(((f32[2,256,1024]{2,1,0:T(8,128)}), f32[2,64,1024]{2,1,0:T(8,128)}) %reduce-scatter.82.cloned.1.call-update) | async-done | bytes 524304 | tf_op jit(solution)/shard_map/reduce_scatter | solution.py:35
  983.5 32.9 %reduce-scatter.74.cloned.1.call-done = f32[2,64,1024]{2,1,0:T(8,128)} async-done(((f32[2,256,1024]{2,1,0:T(8,128)}), f32[2,64,1024]{2,1,0:T(8,128)}) %reduce-scatter.74.cloned.1.call-update) | async-done | bytes 524304 | tf_op jit(solution)/shard_map/reduce_scatter | solution.py:35
  1016.4 34.0 %reduce-scatter.66.cloned.1.call-done = f32[2,64,1024]{2,1,0:T(8,128)} async-done(((f32[2,256,1024]{2,1,0:T(8,128)}), f32[2,64,1024]{2,1,0:T(8,128)}) %reduce-scatter.66.cloned.1.call-update) | async-done | bytes 524304 | tf_op jit(solution)/shard_map/reduce_scatter | solution.py:35
  1050.3 34.0 %reduce-scatter.58.cloned.1.call-done = f32[2,64,1024]{2,1,0:T(8,128)} async-done(((f32[2,256,1024]{2,1,0:T(8,128)}), f32[2,64,1024]{2,1,0:T(8,128)}) %reduce-scatter.58.cloned.1.call-update) | async-done | bytes 524304 | tf_op jit(solution)/shard_map/reduce_scatter | solution.py:35
  1094.6 12.5 all-gather.86.cloned.1.call-done
  1196.5 24.9 %reduce-scatter.84.cloned.1.call-done = bf16[2,256,256]{2,1,0:T(8,128)(2,1)} async-done(((bf16[2,1024,256]{2,1,0:T(8,128)(2,1)}), bf16[2,256,256]{2,1,0:T(8,128)(2,1)}) %reduce-scatter.84.cloned.1.call-update) | async-done | bytes 262160 | tf_op jit(solution)/shard_map/reduce_scatter | solution.py:172
  1230.3 19.0 reduce-scatter.70.cloned.1.call-done
  1249.3 28.2 %reduce-scatter.68.cloned.1.call-done = bf16[2,256,256]{2,1,0:T(8,128)(2,1)} async-done(((bf16[2,1024,256]{2,1,0:T(8,128)(2,1)}), bf16[2,256,256]{2,1,0:T(8,128)(2,1)}) %reduce-scatter.68.cloned.1.call-update) | async-done | bytes 262160 | tf_op jit(solution)/shard_map/reduce_scatter | solution.py:172
  1286.5 19.0 reduce-scatter.62.cloned.1.call-done
  1305.5 28.0 %reduce-scatter.60.cloned.1.call-done = bf16[2,256,256]{2,1,0:T(8,128)(2,1)} async-done(((bf16[2,1024,256]{2,1,0:T(8,128)(2,1)}), bf16[2,256,256]{2,1,0:T(8,128)(2,1)}) %reduce-scatter.60.cloned.1.call-update) | async-done | bytes 262160 | tf_op jit(solution)/shard_map/reduce_scatter | solution.py:172
  1342.6 18.9 reduce-scatter.78.cloned.1.call-done
  1361.5 28.1 %reduce-scatter.76.cloned.1.call-done = bf16[2,256,256]{2,1,0:T(8,128)(2,1)} async-done(((bf16[2,1024,256]{2,1,0:T(8,128)(2,1)}), bf16[2,256,256]{2,1,0:T(8,128)(2,1)}) %reduce-scatter.76.cloned.1.call-update) | async-done | bytes 262160 | tf_op jit(solution)/shard_map/reduce_scatter | solution.py:172
  1393.7 28.9 %reduce-scatter.88.cloned.1.call-done = f32[2,64,1024]{2,1,0:T(8,128)} async-done(((f32[2,256,1024]{2,1,0:T(8,128)}), f32[2,64,1024]{2,1,0:T(8,128)}) %reduce-scatter.88.cloned.1.call-update) | async-done | bytes 524304 | tf_op jit(solution)/shard_map/reduce_scatter | solution.py:35
  1422.7 34.7 %reduce-scatter.72.cloned.1.call-done = f32[2,64,1024]{2,1,0:T(8,128)} async-done(((f32[2,256,1024]{2,1,0:T(8,128)}), f32[2,64,1024]{2,1,0:T(8,128)}) %reduce-scatter.72.cloned.1.call-update) | async-done | bytes 524304 | tf_op jit(solution)/shard_map/reduce_scatter | solution.py:35
  1457.4 33.8 %reduce-scatter.64.cloned.1.call-done = f32[2,64,1024]{2,1,0:T(8,128)} async-done(((f32[2,256,1024]{2,1,0:T(8,128)}), f32[2,64,1024]{2,1,0:T(8,128)}) %reduce-scatter.64.cloned.1.call-update) | async-done | bytes 524304 | tf_op jit(solution)/shard_map/reduce_scatter | solution.py:35
  1491.2 34.2 %reduce-scatter.80.cloned.1.call-done = f32[2,64,1024]{2,1,0:T(8,128)} async-done(((f32[2,256,1024]{2,1,0:T(8,128)}), f32[2,64,1024]{2,1,0:T(8,128)}) %reduce-scatter.80.cloned.1.call-update) | async-done | bytes 524304 | tf_op jit(solution)/shard_map/reduce_scatter | solution.py:35
  1556.3 9.4 all-gather.76.cloned.1.call-done
  1569.0 15.6 all-gather.70.cloned.1.call-done
  1587.9 15.5 all-gather.88.cloned.1.call-done
  1645.5 40.4 %all-reduce.15 = (f32[1024]{0:T(1024)S(1)}, f32[1024]{0:T(1024)S(1)}, f32[1024]{0:T(1024)S(1)}, f32[1024]{0:T(1024)S(1)}, f32[1024]{0:T(1024)S(1)}, /*index=5*/f...) all-reduce(f32[1024]{0:T(1024)S(1)} %dynamic-update-slice.9, ...), channel_id=1, replica_groups=mesh['fsdp'=2,'ctx'=4,'tp'=4] {'fsdp','ctx','tp'}, use_global_device_ids=true, to_apply=%add.6 | all-reduce | flops 12288 | bytes 98304
  1690.6 15.9 reduce-scatter.50.cloned.1.call-done
  1706.5 34.2 %reduce-scatter.56.cloned.1.call-done = f32[2,64,1024]{2,1,0:T(8,128)} async-done(((f32[2,256,1024]{2,1,0:T(8,128)}), f32[2,64,1024]{2,1,0:T(8,128)}) %reduce-scatter.56.cloned.1.call-update) | async-done | bytes 524304 | tf_op jit(solution)/shard_map/reduce_scatter | solution.py:35
  1752.1 59.7 %reduce-scatter.90.cloned.1.call-done = f32[128,2,256]{2,0,1:T(8,128)} async-done(((f32[1024,2,256]{2,0,1:T(8,128)}), f32[128,2,256]{2,0,1:T(8,128)}) %reduce-scatter.90.cloned.1.call-update) | async-done | bytes 262160 | tf_op jit(solution)/shard_map/reduce_scatter | solution.py:40
  1813.7 64.7 %reduce-scatter.94.cloned.1.call-done = f32[128,256]{1,0:T(8,128)} async-done(((f32[1024,256]{1,0:T(8,128)}), f32[128,256]{1,0:T(8,128)}) %reduce-scatter.94.cloned.1.call-update) | async-done | bytes 131088 | tf_op jit(solution)/shard_map/reduce_scatter | solution.py:42
  1878.3 91.6 %reduce-scatter.96.cloned.1.call-done = f32[128,1024]{1,0:T(8,128)} async-done(((f32[1024,1024]{1,0:T(8,128)}), f32[128,1024]{1,0:T(8,128)}) %reduce-scatter.96.cloned.1.call-update) | async-done | bytes 524304 | tf_op jit(solution)/shard_map/reduce_scatter | solution.py:43
  1969.9 91.7 %reduce-scatter.98.cloned.1.call-done = f32[128,1024]{1,0:T(8,128)} async-done(((f32[1024,1024]{1,0:T(8,128)}), f32[128,1024]{1,0:T(8,128)}) %reduce-scatter.98.cloned.1.call-update) | async-done | bytes 524304 | tf_op jit(solution)/shard_map/reduce_scatter | solution.py:44
  2061.6 79.3 %reduce-scatter.92.cloned.1.call-done = f32[128,3,256]{2,0,1:T(8,128)} async-done(((f32[1024,3,256]{2,0,1:T(8,128)}), f32[128,3,256]{2,0,1:T(8,128)}) %reduce-scatter.92.cloned.1.call-update) | async-done | bytes 393232 | tf_op jit(solution)/shard_map/reduce_scatter | solution.py:41
  (737 shorter events, 363.7 us)
Async XLA Ops:
  7.2 46.4 %all-gather.42.cloned.1.call-start = ((), (), s32[]{:S(2)}) async-start(), calls=%async_computation.33 | async-start | bytes 1179648 | tf_op jit(solution)/shard_map/all_gather | solution.py:22
  8.8 96.1 %reduce-scatter.34.cloned.1.call-start = ((), (), s32[]{:S(2)}) async-start(), calls=%async_computation.34 | async-start | bytes 2621440 | tf_op jit(solution)/shard_map/reduce_scatter | solution.py:35
  57.0 65.2 %reduce-scatter.40.cloned.1.call-start = ((), (), s32[]{:S(2)}) async-start(), calls=%async_computation.42 | async-start | bytes 2621440 | tf_op jit(solution)/shard_map/reduce_scatter | solution.py:35
  59.2 96.9 %reduce-scatter.46.cloned.1.call-start = ((), (), s32[]{:S(2)}) async-start(), calls=%async_computation.47 | async-start | bytes 2621440 | tf_op jit(solution)/shard_map/reduce_scatter | solution.py:35
  61.4 128.7 %reduce-scatter.52.cloned.1.call-start = ((), (), s32[]{:S(2)}) async-start(), calls=%async_computation.52 | async-start | bytes 2621440 | tf_op jit(solution)/shard_map/reduce_scatter | solution.py:35
  63.6 174.2 %all-gather.46.cloned.1.call-start = ((), (), s32[]{:S(2)}) async-start(), calls=%async_computation.36 | async-start | bytes 1769472 | tf_op jit(solution)/shard_map/all_gather | solution.py:23
  64.5 190.4 %all-gather.54.cloned.1.call-start = ((), (), s32[]{:S(2)}) async-start(), calls=%async_computation.43 | async-start | bytes 1310720 | tf_op jit(solution)/shard_map/all_gather | solution.py:31
  194.5 79.3 %all-gather.58.cloned.1.call-start = ((), (), s32[]{:S(2)}) async-start(), calls=%async_computation.48 | async-start | bytes 1310720 | tf_op jit(solution)/shard_map/all_gather | solution.py:31
  195.2 97.5 %all-gather.62.cloned.1.call-start = ((), (), s32[]{:S(2)}) async-start(), calls=%async_computation.53 | async-start | bytes 1310720 | tf_op jit(solution)/shard_map/all_gather | solution.py:31
  196.0 115.5 %all-gather.44.cloned.1.call-start = ((), (), s32[]{:S(2)}) async-start(), calls=%async_computation.35 | async-start | bytes 1310720 | tf_op jit(solution)/shard_map/all_gather | solution.py:31
  196.6 154.1 %all-gather.96.cloned.1.call-start = ((), (), s32[]{:S(2)}) async-start(), calls=%async_computation.93 | async-start | bytes 1310720 | tf_op jit(solution)/shard_map/all_gather | solution.py:78
  258.5 122.7 %all-gather.94.cloned.1.call-start = ((), (), s32[]{:S(2)}) async-start(), calls=%async_computation.92 | async-start | bytes 1310720 | tf_op jit(solution)/shard_map/all_gather | solution.py:79
  259.1 152.8 %all-gather.100.cloned.1.call-start = ((), (), s32[]{:S(2)}) async-start(), calls=%async_computation.95 | async-start | bytes 1310720 | tf_op jit(solution)/shard_map/all_gather | solution.py:78
  277.4 165.0 %all-gather.98.cloned.1.call-start = ((), (), s32[]{:S(2)}) async-start(), calls=%async_computation.94 | async-start | bytes 1310720 | tf_op jit(solution)/shard_map/all_gather | solution.py:79
  278.0 194.9 %all-gather.104.cloned.1.call-start = ((), (), s32[]{:S(2)}) async-start(), calls=%async_computation.97 | async-start | bytes 1310720 | tf_op jit(solution)/shard_map/all_gather | solution.py:78
  296.4 206.6 %all-gather.102.cloned.1.call-start = ((), (), s32[]{:S(2)}) async-start(), calls=%async_computation.96 | async-start | bytes 1310720 | tf_op jit(solution)/shard_map/all_gather | solution.py:79
  296.9 236.5 %all-gather.92.cloned.1.call-start = ((), (), s32[]{:S(2)}) async-start(), calls=%async_computation.91 | async-start | bytes 1310720 | tf_op jit(solution)/shard_map/all_gather | solution.py:78
  315.1 248.3 %all-gather.90.cloned.1.call-start = ((), (), s32[]{:S(2)}) async-start(), calls=%async_computation.90 | async-start | bytes 1310720 | tf_op jit(solution)/shard_map/all_gather | solution.py:79
  350.1 246.2 %reduce-scatter.42.cloned.1.call-start = ((), (), s32[]{:S(2)}) async-start(), calls=%async_computation.44 | async-start | bytes 2621440 | tf_op jit(solution)/shard_map/reduce_scatter | solution.py:35
  388.4 242.4 %reduce-scatter.48.cloned.1.call-start = ((), (), s32[]{:S(2)}) async-start(), calls=%async_computation.49 | async-start | bytes 2621440 | tf_op jit(solution)/shard_map/reduce_scatter | solution.py:35
  449.6 215.2 %reduce-scatter.54.cloned.1.call-start = ((), (), s32[]{:S(2)}) async-start(), calls=%async_computation.54 | async-start | bytes 2621440 | tf_op jit(solution)/shard_map/reduce_scatter | solution.py:35
  510.1 188.9 %reduce-scatter.36.cloned.1.call-start = ((), (), s32[]{:S(2)}) async-start(), calls=%async_computation.37 | async-start | bytes 2621440 | tf_op jit(solution)/shard_map/reduce_scatter | solution.py:35
  570.6 182.3 %all-gather.50.cloned.1.call-start = ((), (), s32[]{:S(2)}) async-start(), calls=%async_computation.39 | async-start | bytes 2359296 | tf_op jit(solution)/shard_map/all_gather | solution.py:25
  571.3 196.4 %all-gather.60.cloned.1.call-start = ((), (), s32[]{:S(2)}) async-start(), calls=%async_computation.50 | async-start | bytes 1310720 | tf_op jit(solution)/shard_map/all_gather | solution.py:31
  703.7 82.9 %all-gather.64.cloned.1.call-start = ((), (), s32[]{:S(2)}) async-start(), calls=%async_computation.55 | async-start | bytes 1310720 | tf_op jit(solution)/shard_map/all_gather | solution.py:31
  704.4 100.9 %all-gather.56.cloned.1.call-start = ((), (), s32[]{:S(2)}) async-start(), calls=%async_computation.45 | async-start | bytes 1310720 | tf_op jit(solution)/shard_map/all_gather | solution.py:31
  705.0 119.1 %all-gather.48.cloned.1.call-start = ((), (), s32[]{:S(2)}) async-start(), calls=%async_computation.38 | async-start | bytes 1310720 | tf_op jit(solution)/shard_map/all_gather | solution.py:31
  705.6 149.5 %all-gather.84.cloned.1.call-start = ((), (), s32[]{:S(2)}) async-start(), calls=%async_computation.78 | async-start | bytes 1310720 | tf_op jit(solution)/shard_map/all_gather | solution.py:31
  709.0 184.9 %all-gather.52.cloned.1.call-start = ((), (), s32[]{:S(2)}) async-start(), calls=%async_computation.40 | async-start | bytes 2359296 | tf_op jit(solution)/shard_map/all_gather | solution.py:26
  709.7 200.8 %all-gather.78.cloned.1.call-start = ((), (), s32[]{:S(2)}) async-start(), calls=%async_computation.71 | async-start | bytes 1310720 | tf_op jit(solution)/shard_map/all_gather | solution.py:31
  710.3 218.6 %all-gather.72.cloned.1.call-start = ((), (), s32[]{:S(2)}) async-start(), calls=%async_computation.64 | async-start | bytes 1310720 | tf_op jit(solution)/shard_map/all_gather | solution.py:31
  711.0 236.2 %all-gather.66.cloned.1.call-start = ((), (), s32[]{:S(2)}) async-start(), calls=%async_computation.57 | async-start | bytes 1310720 | tf_op jit(solution)/shard_map/all_gather | solution.py:31
  711.8 269.8 %reduce-scatter.82.cloned.1.call-start = ((), (), s32[]{:S(2)}) async-start(), calls=%async_computation.79 | async-start | bytes 2621440 | tf_op jit(solution)/shard_map/reduce_scatter | solution.py:35
  903.3 113.0 %reduce-scatter.74.cloned.1.call-start = ((), (), s32[]{:S(2)}) async-start(), calls=%async_computation.72 | async-start | bytes 2621440 | tf_op jit(solution)/shard_map/reduce_scatter | solution.py:35
  920.0 130.4 %reduce-scatter.66.cloned.1.call-start = ((), (), s32[]{:S(2)}) async-start(), calls=%async_computation.65 | async-start | bytes 2621440 | tf_op jit(solution)/shard_map/reduce_scatter | solution.py:35
  938.3 146.0 %reduce-scatter.58.cloned.1.call-start = ((), (), s32[]{:S(2)}) async-start(), calls=%async_computation.58 | async-start | bytes 2621440 | tf_op jit(solution)/shard_map/reduce_scatter | solution.py:35
  956.7 150.4 %all-gather.86.cloned.1.call-start = ((), (), s32[]{:S(2)}) async-start(), calls=%async_computation.80 | async-start | bytes 1310720 | tf_op jit(solution)/shard_map/all_gather | solution.py:31
  1090.2 38.6 %all-gather.74.cloned.1.call-start = ((), (), s32[]{:S(2)}) async-start(), calls=%async_computation.66 | async-start | bytes 1310720 | tf_op jit(solution)/shard_map/all_gather | solution.py:31
  1093.2 56.8 %all-gather.68.cloned.1.call-start = ((), (), s32[]{:S(2)}) async-start(), calls=%async_computation.59 | async-start | bytes 1310720 | tf_op jit(solution)/shard_map/all_gather | solution.py:31
  1093.8 77.7 %all-gather.80.cloned.1.call-start = ((), (), s32[]{:S(2)}) async-start(), calls=%async_computation.73 | async-start | bytes 1310720 | tf_op jit(solution)/shard_map/all_gather | solution.py:31
  1094.6 101.9 %reduce-scatter.86.cloned.1.call-start = ((), (), s32[]{:S(2)}) async-start(), calls=%async_computation.82 | async-start | bytes 1310720 | tf_op jit(solution)/shard_map/reduce_scatter | solution.py:178
  1115.1 106.2 %reduce-scatter.84.cloned.1.call-start = ((), (), s32[]{:S(2)}) async-start(), calls=%async_computation.81 | async-start | bytes 1310720 | tf_op jit(solution)/shard_map/reduce_scatter | solution.py:172
  1128.3 121.0 %reduce-scatter.70.cloned.1.call-start = ((), (), s32[]{:S(2)}) async-start(), calls=%async_computation.68 | async-start | bytes 1310720 | tf_op jit(solution)/shard_map/reduce_scatter | solution.py:178
  1137.0 140.5 %reduce-scatter.68.cloned.1.call-start = ((), (), s32[]{:S(2)}) async-start(), calls=%async_computation.67 | async-start | bytes 1310720 | tf_op jit(solution)/shard_map/reduce_scatter | solution.py:172
  1150.0 155.5 %reduce-scatter.62.cloned.1.call-start = ((), (), s32[]{:S(2)}) async-start(), calls=%async_computation.61 | async-start | bytes 1310720 | tf_op jit(solution)/shard_map/reduce_scatter | solution.py:178
  1158.4 175.1 %reduce-scatter.60.cloned.1.call-start = ((), (), s32[]{:S(2)}) async-start(), calls=%async_computation.60 | async-start | bytes 1310720 | tf_op jit(solution)/shard_map/reduce_scatter | solution.py:172
  1171.3 190.2 %reduce-scatter.78.cloned.1.call-start = ((), (), s32[]{:S(2)}) async-start(), calls=%async_computation.75 | async-start | bytes 1310720 | tf_op jit(solution)/shard_map/reduce_scatter | solution.py:178
  1179.7 209.9 %reduce-scatter.76.cloned.1.call-start = ((), (), s32[]{:S(2)}) async-start(), calls=%async_computation.74 | async-start | bytes 1310720 | tf_op jit(solution)/shard_map/reduce_scatter | solution.py:172
  1192.6 230.0 %reduce-scatter.88.cloned.1.call-start = ((), (), s32[]{:S(2)}) async-start(), calls=%async_computation.83 | async-start | bytes 2621440 | tf_op jit(solution)/shard_map/reduce_scatter | solution.py:35
  1225.2 232.2 %reduce-scatter.72.cloned.1.call-start = ((), (), s32[]{:S(2)}) async-start(), calls=%async_computation.69 | async-start | bytes 2621440 | tf_op jit(solution)/shard_map/reduce_scatter | solution.py:35
  1281.4 209.8 %reduce-scatter.64.cloned.1.call-start = ((), (), s32[]{:S(2)}) async-start(), calls=%async_computation.62 | async-start | bytes 2621440 | tf_op jit(solution)/shard_map/reduce_scatter | solution.py:35
  1337.5 187.9 %reduce-scatter.80.cloned.1.call-start = ((), (), s32[]{:S(2)}) async-start(), calls=%async_computation.76 | async-start | bytes 2621440 | tf_op jit(solution)/shard_map/reduce_scatter | solution.py:35
  1393.7 158.4 %all-gather.82.cloned.1.call-start = ((), (), s32[]{:S(2)}) async-start(), calls=%async_computation.77 | async-start | bytes 1310720 | tf_op jit(solution)/shard_map/all_gather | solution.py:31
  1532.6 51.9 %all-gather.70.cloned.1.call-start = ((), (), s32[]{:S(2)}) async-start(), calls=%async_computation.63 | async-start | bytes 1310720 | tf_op jit(solution)/shard_map/all_gather | solution.py:31
  1534.7 68.7 %all-gather.88.cloned.1.call-start = ((), (), s32[]{:S(2)}) async-start(), calls=%async_computation.84 | async-start | bytes 1310720 | tf_op jit(solution)/shard_map/all_gather | solution.py:31
  1535.9 154.6 %reduce-scatter.38.cloned.1.call-start = ((), (), s32[]{:S(2)}) async-start(), calls=%async_computation.41 | async-start | bytes 2621440 | tf_op jit(solution)/shard_map/reduce_scatter | solution.py:35
  1540.4 150.1 %reduce-scatter.44.cloned.1.call-start = ((), (), s32[]{:S(2)}) async-start(), calls=%async_computation.46 | async-start | bytes 2621440 | tf_op jit(solution)/shard_map/reduce_scatter | solution.py:35
  1544.3 162.2 %reduce-scatter.50.cloned.1.call-start = ((), (), s32[]{:S(2)}) async-start(), calls=%async_computation.51 | async-start | bytes 2621440 | tf_op jit(solution)/shard_map/reduce_scatter | solution.py:35
  1548.1 192.5 %reduce-scatter.56.cloned.1.call-start = ((), (), s32[]{:S(2)}) async-start(), calls=%async_computation.56 | async-start | bytes 2621440 | tf_op jit(solution)/shard_map/reduce_scatter | solution.py:35
  1552.0 259.8 %reduce-scatter.90.cloned.1.call-start = ((), (), s32[]{:S(2)}) async-start(), calls=%async_computation.85 | async-start | bytes 2359296 | tf_op jit(solution)/shard_map/reduce_scatter | solution.py:40
  1608.8 269.6 %reduce-scatter.94.cloned.1.call-start = ((), (), s32[]{:S(2)}) async-start(), calls=%async_computation.87 | async-start | bytes 1179648 | tf_op jit(solution)/shard_map/reduce_scatter | solution.py:42
  1615.1 354.7 %reduce-scatter.96.cloned.1.call-start = ((), (), s32[]{:S(2)}) async-start(), calls=%async_computation.88 | async-start | bytes 4718592 | tf_op jit(solution)/shard_map/reduce_scatter | solution.py:43
  1624.7 436.9 %reduce-scatter.98.cloned.1.call-start = ((), (), s32[]{:S(2)}) async-start(), calls=%async_computation.89 | async-start | bytes 4718592 | tf_op jit(solution)/shard_map/reduce_scatter | solution.py:44
  1635.1 505.9 %reduce-scatter.92.cloned.1.call-start = ((), (), s32[]{:S(2)}) async-start(), calls=%async_computation.86 | async-start | bytes 3538944 | tf_op jit(solution)/shard_map/reduce_scatter | solution.py:41
  (194 other events, 8016.3 us)
Sparse Core Ops, SparseCore 0:
  10.7 42.8 all-gather.41
  57.1 30.3 reduce-scatter.33
  90.8 31.4 reduce-scatter.39
  124.7 31.3 reduce-scatter.45
  158.6 31.4 reduce-scatter.51
  192.5 45.3 all-gather.45
  257.1 16.7 all-gather.57
  276.0 16.7 all-gather.61
  294.7 16.7 all-gather.43
  313.6 37.0 all-gather.95
  352.7 28.5 all-gather.93
  383.4 28.4 all-gather.99
  413.9 28.4 all-gather.97
  444.4 28.4 all-gather.103
  474.4 28.4 all-gather.101
  504.9 28.4 all-gather.91
  534.9 28.4 all-gather.89
  566.5 29.7 reduce-scatter.41
  599.3 31.4 reduce-scatter.47
  633.4 31.3 reduce-scatter.53
  667.5 31.4 reduce-scatter.35
  701.1 49.2 all-gather.49
  752.4 15.2 all-gather.59
  769.8 16.7 all-gather.63
  788.6 16.7 all-gather.55
  807.3 16.7 all-gather.47
  825.7 16.7 all-gather.83
  844.6 49.2 all-gather.51
  895.3 15.1 all-gather.77
  912.1 16.7 all-gather.71
  930.5 16.7 all-gather.65
  950.2 31.4 reduce-scatter.81
  984.9 31.4 reduce-scatter.73
  1018.9 31.4 reduce-scatter.65
  1052.9 31.4 reduce-scatter.57
  1090.3 16.7 all-gather.85
  1108.6 16.7 all-gather.73
  1126.8 16.7 all-gather.67
  1145.7 16.7 all-gather.79
  1165.3 27.1 reduce-scatter.85
  1195.5 25.7 reduce-scatter.83
  1223.5 25.8 reduce-scatter.69
  1251.7 25.7 reduce-scatter.67
  1279.7 25.8 reduce-scatter.61
  1307.8 25.7 reduce-scatter.59
  1335.7 25.7 reduce-scatter.77
  1363.8 25.7 reduce-scatter.75
  1392.6 30.0 reduce-scatter.87
  1425.9 31.4 reduce-scatter.71
  1459.8 31.4 reduce-scatter.63
  1493.9 31.4 reduce-scatter.79
  1530.6 16.7 all-gather.81
  1548.9 16.7 all-gather.75
  1567.8 16.7 all-gather.69
  1586.7 16.7 all-gather.87
  1606.5 31.4 reduce-scatter.37
  1641.1 31.5 reduce-scatter.43
  1675.1 31.3 reduce-scatter.49
  1709.2 31.4 reduce-scatter.55
  1744.2 67.5 reduce-scatter.89
  1815.8 62.4 reduce-scatter.93
  1882.8 87.0 reduce-scatter.95
  1973.9 87.6 reduce-scatter.97
  2066.2 74.6 reduce-scatter.91
  (1 shorter events, 14.8 us)
where the time goes:
time: 2160 us; the launch traced here: 2150 us
  waiting for transfers between devices  1570 us (73%)
  matrix products  256 us (12%)
  blocking collectives  155 us (7%)
  other arithmetic  86.4 us (4%)
  local copies, waits for them, and re-layouts  58.5 us (3%)
    reduce_scatter x20, waiting for transfers between devices, fold_rows(): return lax.psum_scatter(block, 'tp', scatter_dimension=1, tiled=True)  519 us
    all_gather x20, waiting for transfers between devices, spread_rows(): return lax.all_gather(block, 'tp', axis=1, tiled=True)  196 us
    reduce_scatter x4, waiting for transfers between devices, micro_step(): lax.psum_scatter(key_terms.reshape(groups, seq_len, heads_dev * HD).astyp...  109 us
    all_gather x4, waiting for transfers between devices, micro_step(): lax.all_gather(project[:, :, 2], 'ctx', axis=1, tiled=True)  97.3 us
    reduce_scatter x1, waiting for transfers between devices, reduce_weights(): lax.psum_scatter(parts[4], ('fsdp', 'ctx'), scatter_dimension=0, tiled=True)  91.7 us
    reduce_scatter x1, waiting for transfers between devices, reduce_weights(): lax.psum_scatter(parts[3], ('fsdp', 'ctx'), scatter_dimension=0, tiled=True)  91.6 us
    reduce_scatter x1, waiting for transfers between devices, reduce_weights(): lax.psum_scatter(parts[1], ('fsdp', 'ctx'), scatter_dimension=0, tiled=True)  79.3 us
    unnamed x2, blocking collectives  79.3 us
  transfers between devices with their start and end apart: 65, of which 55 were waited for; matrix products, arithmetic and copies ran while one was open for 16% of the time, Pallas kernels for 0%

commit v1 on v0

--- a/solution.py
+++ b/solution.py
@@ -5,6 +5,19 @@
 
 HD = 64
 EPSILON = 1e-05
+
+
+def ring_gather(array, axis, dim):
+    ways = lax.axis_size(axis)
+    up = [(d, (d + 1) % ways) for d in range(ways)]
+    down = [(d, (d - 1) % ways) for d in range(ways)]
+    earlier, later = ([array], [array])
+    for _ in range(ways // 2):
+        earlier.append(lax.ppermute(earlier[-1], axis, up))
+    for _ in range((ways - 1) // 2):
+        later.append(lax.ppermute(later[-1], axis, down))
+    line = jnp.concatenate([*earlier[::-1], *later[1:]], axis=dim)
+    return jnp.roll(line, (lax.axis_index(axis) - ways // 2) * array.shape[dim], axis=dim)
 
 
 def layer_norm(matrix, scales, shifts):
@@ -28,7 +41,7 @@
 
 
 def spread_rows(block):
-    return lax.all_gather(block, "tp", axis=1, tiled=True)
+    return ring_gather(block, "tp", 1)
 
 
 def fold_rows(block):

time: 2160 us -> 1840 us (0.85)
  waiting for transfers between devices: 1570 us -> 1170 us
  other arithmetic: 86.4 us -> 136 us
  starting transfers between devices: 4.62 us -> 49.4 us
  matrix products: 256 us -> 233 us
    all_gather x20 -> x0, waiting for transfers between devices: 196 us -> none  [spread_rows(): return lax.all_gather(block, 'tp', axis=1, tiled=True)]
    ppermute x0 -> x60, waiting for transfers between devices: none -> 163 us  [the longest x40 162 us: ring_gather(): earlier.append(lax.ppermute(earlier[-1], axis, up))]
    reduce_scatter x20, waiting for transfers between devices: 519 us -> 379 us  [fold_rows(): return lax.psum_scatter(block, 'tp', scatter_dimension=1, tiled=True)]
    reduce_scatter x4, waiting for transfers between devices: 109 us -> 44.6 us  [micro_step(): lax.psum_scatter(key_terms.reshape(groups, seq_len, heads_dev * HD).astyp...]
    ppermute x0 -> x60, starting transfers between devices: none -> 46.3 us  [the longest x20 30.3 us: ring_gather(): later.append(lax.ppermute(later[-1], axis, down))]
    concatenate x0 -> x15, other arithmetic: none -> 45.9 us  [ring_gather(): jnp.roll(line, (lax.axis_index(axis) - ways // 2) * array.shape[dim], axi...]
    all_gather x1, waiting for transfers between devices: 38.8 us -> 0.01 us  [fetch(): lax.all_gather(shrink_part, ('fsdp', 'ctx'), axis=0, tiled=True)]
    reduce_scatter x4, waiting for transfers between devices: 57 us -> 19.1 us  [micro_step(): lax.psum_scatter(value_terms.reshape(groups, seq_len, heads_dev * HD).ast...]
  transfers between devices with their start and end apart: 65 -> 105, of which waited for: 55 -> 64; matrix products, arithmetic and copies ran while one was open for 16% -> 20% of each run, Pallas kernels for 0% -> 0%
where the time goes in v1:
time: 1840 us; the launch traced here: 1830 us
  waiting for transfers between devices  1170 us (64%)
  matrix products  233 us (13%)
  blocking collectives  156 us (8%)
  other arithmetic  136 us (7%)
  local copies, waits for them, and re-layouts  68.4 us (4%)
  starting transfers between devices  49.4 us (3%)
    reduce_scatter x20, waiting for transfers between devices, fold_rows(): return lax.psum_scatter(block, 'tp', scatter_dimension=1, tiled=True)  379 us
    ppermute x40, waiting for transfers between devices, ring_gather(): earlier.append(lax.ppermute(earlier[-1], axis, up))  162 us
    reduce_scatter x1, waiting for transfers between devices, reduce_weights(): lax.psum_scatter(parts[4], ('fsdp', 'ctx'), scatter_dimension=0, tiled=True)  91.9 us
    reduce_scatter x1, waiting for transfers between devices, reduce_weights(): lax.psum_scatter(parts[3], ('fsdp', 'ctx'), scatter_dimension=0, tiled=True)  91.4 us
    unnamed x2, blocking collectives  79.4 us
    reduce_scatter x1, waiting for transfers between devices, reduce_weights(): lax.psum_scatter(parts[1], ('fsdp', 'ctx'), scatter_dimension=0, tiled=True)  79.3 us
    reduce_scatter x1, waiting for transfers between devices, reduce_weights(): lax.psum_scatter(parts[2], ('fsdp', 'ctx'), scatter_dimension=0, tiled=True)  64.6 us
    reduce_scatter x1, waiting for transfers between devices, reduce_weights(): lax.psum_scatter(parts[0], ('fsdp', 'ctx'), scatter_dimension=0, tiled=True)  60.2 us
  transfers between devices with their start and end apart: 105, of which 64 were waited for; matrix products, arithmetic and copies ran while one was open for 20% of the time, Pallas kernels for 0%

profile of v1, /device:TPU:0, one launch (start us, length us, event | category | flops | bytes accessed | tf_op | source)
XLA Modules:
  0.0 1834.1 jit_solution(9446345232508961079)
XLA Ops:
  10.6 43.0 %all-gather.22.cloned.1.call-done = bf16[1024,2,256]{2,0,1:T(8,128)(2,1)} async-done(((bf16[128,2,256]{2,0,1:T(8,128)(2,1)}), bf16[1024,2,256]{2,0,1:T(8,128)(2,1)}) %all-gather.22.cloned.1.call-update) | async-done | bytes 1048592 | tf_op jit(solution)/shard_map/all_gather | solution.py:35
  65.9 38.9 %all-reduce.16 = (f32[1024]{0:T(1024)S(1)}, f32[1024]{0:T(1024)S(1)}, f32[1024]{0:T(1024)S(1)}, f32[1024]{0:T(1024)S(1)}, f32[1024]{0:T(1024)S(1)}, /*index=5*/f32[1024]{0:T(1024)S(1)}) all-reduce(f32[1024]{0:T(1024)S(1)} %dynamic-update-slice.3, ...), channel_id=1, replica_groups=mesh['fsdp'=2,'ctx'=4,'tp'=4] {'fsdp','ctx','tp'}, use_global_device_ids=true, to_apply=%add | all-reduce | flops 6144 | bytes 49152
  106.2 16.1 reduce-scatter.40.cloned.1.call-done
  122.3 33.8 %reduce-scatter.46.cloned.1.call-done = f32[2,64,1024]{2,1,0:T(8,128)} async-done(((f32[2,256,1024]{2,1,0:T(8,128)}), f32[2,64,1024]{2,1,0:T(8,128)}) %reduce-scatter.46.cloned.1.call-update) | async-done | bytes 524304 | tf_op jit(solution)/shard_map/reduce_scatter | solution.py:48
  156.1 34.0 %reduce-scatter.52.cloned.1.call-done = f32[2,64,1024]{2,1,0:T(8,128)} async-done(((f32[2,256,1024]{2,1,0:T(8,128)}), f32[2,64,1024]{2,1,0:T(8,128)}) %reduce-scatter.52.cloned.1.call-update) | async-done | bytes 524304 | tf_op jit(solution)/shard_map/reduce_scatter | solution.py:48
  195.3 6.3 collective-permute-done.6
  201.6 5.8 collective-permute-done.7
  210.2 27.7 %all-gather.24.cloned.1.call-done = bf16[1024,3,256]{0,2,1:T(8,128)(2,1)} async-done(((bf16[128,3,256]{0,2,1:T(8,128)(2,1)}), bf16[1024,3,256]{0,2,1:T(8,128)(2,1)}) %all-gather.24.cloned.1.call-update) | async-done | bytes 1572880 | tf_op jit(solution)/shard_map/all_gather | solution.py:36
  301.1 35.3 %all_gather.85 = bf16[1024,256]{1,0:T(8,128)(2,1)S(1)} all-gather(bf16[128,256]{1,0:T(8,128)(2,1)S(1)} %copy-done.151), channel_id=1, replica_groups=mesh['fsdp'=2,'ctx'=4,'tp'=4] {'fsdp','ctx'}, dimensions={0}, use_global_device_ids=true | all-gather | bytes 589824 | tf_op jit(solution)/shard_map/all_gather | solution.py:37
  342.4 5.6 convolution_convert_fusion.10
  356.1 11.5 all-gather.38.cloned.1.call-done
  367.6 5.3 convolution_convert_fusion.9
  374.8 23.4 %all-gather.44.cloned.1.call-done = bf16[2,1024,1,256]{1,3,2,0:T(8,128)(2,1)} async-done(((bf16[2,256,1,256]{1,3,2,0:T(8,128)(2,1)}), bf16[2,1024,1,256]{1,3,2,0:T(8,128)(2,1)}) %all-gather.44.cloned.1.call-update) | async-done | bytes 1048592 | tf_op jit(solution)/shard_map/all_gather | solution.py:91
  404.1 24.1 %all-gather.42.cloned.1.call-done = bf16[2,1024,1,256]{1,3,2,0:T(8,128)(2,1)} async-done(((bf16[2,256,1,256]{1,3,2,0:T(8,128)(2,1)}), bf16[2,1024,1,256]{1,3,2,0:T(8,128)(2,1)}) %all-gather.42.cloned.1.call-update) | async-done | bytes 1048592 | tf_op jit(solution)/shard_map/all_gather | solution.py:92
  428.2 5.3 convolution_convert_fusion.8
  435.6 22.7 %all-gather.32.cloned.1.call-done = bf16[2,1024,1,256]{1,3,2,0:T(8,128)(2,1)} async-done(((bf16[2,256,1,256]{1,3,2,0:T(8,128)(2,1)}), bf16[2,1024,1,256]{1,3,2,0:T(8,128)(2,1)}) %all-gather.32.cloned.1.call-update) | async-done | bytes 1048592 | tf_op jit(solution)/shard_map/all_gather | solution.py:91
  464.3 24.0 %all-gather.30.cloned.1.call-done = bf16[2,1024,1,256]{1,3,2,0:T(8,128)(2,1)} async-done(((bf16[2,256,1,256]{1,3,2,0:T(8,128)(2,1)}), bf16[2,1024,1,256]{1,3,2,0:T(8,128)(2,1)}) %all-gather.30.cloned.1.call-update) | async-done | bytes 1048592 | tf_op jit(solution)/shard_map/all_gather | solution.py:92
  488.3 5.3 convolution_convert_fusion.11
  498.3 22.6 %reduce-scatter.42.cloned.1.call-done = f32[2,64,1024]{2,1,0:T(8,128)} async-done(((f32[2,256,1024]{2,1,0:T(8,128)}), f32[2,64,1024]{2,1,0:T(8,128)}) %reduce-scatter.42.cloned.1.call-update) | async-done | bytes 524304 | tf_op jit(solution)/shard_map/reduce_scatter | solution.py:48
  520.9 34.6 %reduce-scatter.48.cloned.1.call-done = f32[2,64,1024]{2,1,0:T(8,128)} async-done(((f32[2,256,1024]{2,1,0:T(8,128)}), f32[2,64,1024]{2,1,0:T(8,128)}) %reduce-scatter.48.cloned.1.call-update) | async-done | bytes 524304 | tf_op jit(solution)/shard_map/reduce_scatter | solution.py:48
  555.5 33.8 %reduce-scatter.54.cloned.1.call-done = f32[2,64,1024]{2,1,0:T(8,128)} async-done(((f32[2,256,1024]{2,1,0:T(8,128)}), f32[2,64,1024]{2,1,0:T(8,128)}) %reduce-scatter.54.cloned.1.call-update) | async-done | bytes 524304 | tf_op jit(solution)/shard_map/reduce_scatter | solution.py:48
  589.3 34.0 %reduce-scatter.36.cloned.1.call-done = f32[2,64,1024]{2,1,0:T(8,128)} async-done(((f32[2,256,1024]{2,1,0:T(8,128)}), f32[2,64,1024]{2,1,0:T(8,128)}) %reduce-scatter.36.cloned.1.call-update) | async-done | bytes 524304 | tf_op jit(solution)/shard_map/reduce_scatter | solution.py:48
  629.6 41.6 %all-gather.8 = f32[32,1,128]{2,1,0:T(1,128)S(1)} all-gather(f32[1,1,128]{2,1,0:T(1,128)S(1)} %bitcast.619), channel_id=1, replica_groups=mesh['fsdp'=2,'ctx'=4,'tp'=4] {'fsdp','ctx','tp'}, dimensions={0}, use_global_device_ids=true | all-gather | bytes 16896 | tf_op jit(solution)/shard_map/all_gather | solution.py:267
  710.9 5.8 fusion.300
  718.1 21.2 %multiply_convert_fusion.9 = (bf16[2,256,1024]{2,1,0:T(8,128)(2,1)}, f32[2,256,1024]{2,1,0:T(8,128)}, bf16[2,256,1024]{2,1,0:T(8,128)(2,1)}, f32[2,256,1024]{2,1...) fusion(f32[2,256,1024]{2,1,0:T(8,128)S(1)} %fusion.34, ...), kind=kLoop, calls=%fused_computation.280 | loop fusion | flops 147324928 | bytes 23072768 | tf_op jit(solution)/shard_map/convert_element_type | solution.py:124
  739.2 5.8 convert_reduce_fusion
  751.3 5.9 collective-permute-done.42
  757.4 5.8 collective-permute-done.43
  777.4 6.6 collective-permute-done.33
  784.0 5.8 collective-permute-done.34
  792.6 5.2 convert_reduce_fusion.2
  803.6 11.5 collective-permute-done.24
  815.1 7.2 collective-permute-done.25
  825.1 5.2 convert_reduce_fusion.3
  835.9 20.4 %reduce-scatter.66.cloned.1.call-done = f32[2,64,1024]{2,1,0:T(8,128)} async-done(((f32[2,256,1024]{2,1,0:T(8,128)}), f32[2,64,1024]{2,1,0:T(8,128)}) %reduce-scatter.66.cloned.1.call-update) | async-done | bytes 524304 | tf_op jit(solution)/shard_map/reduce_scatter | solution.py:48
  856.3 34.0 %reduce-scatter.58.cloned.1.call-done = f32[2,64,1024]{2,1,0:T(8,128)} async-done(((f32[2,256,1024]{2,1,0:T(8,128)}), f32[2,64,1024]{2,1,0:T(8,128)}) %reduce-scatter.58.cloned.1.call-update) | async-done | bytes 524304 | tf_op jit(solution)/shard_map/reduce_scatter | solution.py:48
  899.2 6.3 collective-permute-done.54
  905.7 5.8 collective-permute-done.55
  919.8 6.0 multiply_reduce_fusion
  936.9 5.9 collective-permute-done.36
  943.0 5.8 collective-permute-done.37
  952.0 6.2 convolution_convert_fusion.2
  981.3 5.2 collective-permute-done.28
  989.8 6.1 convolution_convert_fusion.3
  1013.0 5.4 collective-permute-done.45
  1018.5 5.8 collective-permute-done.46
  1027.5 6.1 convolution_convert_fusion.1
  1071.4 16.4 reduce-scatter.60.cloned.1.call-done
  1096.9 19.0 %reduce-scatter.78.cloned.1.call-done = bf16[2,256,256]{2,1,0:T(8,128)(2,1)} async-done(((bf16[2,1024,256]{2,1,0:T(8,128)(2,1)}), bf16[2,256,256]{2,1,0:T(8,128)(2,1)}) %reduce-scatter.78.cloned.1.call-update) | async-done | bytes 262160 | tf_op jit(solution)/shard_map/reduce_scatter | solution.py:191
  1115.9 28.2 %reduce-scatter.76.cloned.1.call-done = bf16[2,256,256]{2,1,0:T(8,128)(2,1)} async-done(((bf16[2,1024,256]{2,1,0:T(8,128)(2,1)}), bf16[2,256,256]{2,1,0:T(8,128)(2,1)}) %reduce-scatter.76.cloned.1.call-update) | async-done | bytes 262160 | tf_op jit(solution)/shard_map/reduce_scatter | solution.py:185
  1170.1 7.1 reduce-scatter.88.cloned.1.call-done
  1177.2 34.1 %reduce-scatter.72.cloned.1.call-done = f32[2,64,1024]{2,1,0:T(8,128)} async-done(((f32[2,256,1024]{2,1,0:T(8,128)}), f32[2,64,1024]{2,1,0:T(8,128)}) %reduce-scatter.72.cloned.1.call-update) | async-done | bytes 524304 | tf_op jit(solution)/shard_map/reduce_scatter | solution.py:48
  1211.3 34.0 %reduce-scatter.64.cloned.1.call-done = f32[2,64,1024]{2,1,0:T(8,128)} async-done(((f32[2,256,1024]{2,1,0:T(8,128)}), f32[2,64,1024]{2,1,0:T(8,128)}) %reduce-scatter.64.cloned.1.call-update) | async-done | bytes 524304 | tf_op jit(solution)/shard_map/reduce_scatter | solution.py:48
  1245.3 34.0 %reduce-scatter.80.cloned.1.call-done = f32[2,64,1024]{2,1,0:T(8,128)} async-done(((f32[2,256,1024]{2,1,0:T(8,128)}), f32[2,64,1024]{2,1,0:T(8,128)}) %reduce-scatter.80.cloned.1.call-update) | async-done | bytes 524304 | tf_op jit(solution)/shard_map/reduce_scatter | solution.py:48
  1296.2 5.9 collective-permute-done.58
  1306.8 5.7 collective-permute-done.39
  1312.5 9.5 collective-permute-done.30
  1374.5 40.5 %all-reduce.15 = (f32[1024]{0:T(1024)S(1)}, f32[1024]{0:T(1024)S(1)}, f32[1024]{0:T(1024)S(1)}, f32[1024]{0:T(1024)S(1)}, f32[1024]{0:T(1024)S(1)}, /*index=5*/f...) all-reduce(f32[1024]{0:T(1024)S(1)} %dynamic-update-slice.9, ...), channel_id=1, replica_groups=mesh['fsdp'=2,'ctx'=4,'tp'=4] {'fsdp','ctx','tp'}, use_global_device_ids=true, to_apply=%add.6 | all-reduce | flops 12288 | bytes 98304
  1419.7 6.7 reduce-scatter.56.cloned.1.call-done
  1437.8 60.2 %reduce-scatter.90.cloned.1.call-done = f32[128,2,256]{2,0,1:T(8,128)} async-done(((f32[1024,2,256]{2,0,1:T(8,128)}), f32[128,2,256]{2,0,1:T(8,128)}) %reduce-scatter.90.cloned.1.call-update) | async-done | bytes 262160 | tf_op jit(solution)/shard_map/reduce_scatter | solution.py:53
  1499.9 64.6 %reduce-scatter.94.cloned.1.call-done = f32[128,256]{1,0:T(8,128)} async-done(((f32[1024,256]{1,0:T(8,128)}), f32[128,256]{1,0:T(8,128)}) %reduce-scatter.94.cloned.1.call-update) | async-done | bytes 131088 | tf_op jit(solution)/shard_map/reduce_scatter | solution.py:55
  1564.5 91.4 %reduce-scatter.96.cloned.1.call-done = f32[128,1024]{1,0:T(8,128)} async-done(((f32[1024,1024]{1,0:T(8,128)}), f32[128,1024]{1,0:T(8,128)}) %reduce-scatter.96.cloned.1.call-update) | async-done | bytes 524304 | tf_op jit(solution)/shard_map/reduce_scatter | solution.py:56
  1655.9 91.9 %reduce-scatter.98.cloned.1.call-done = f32[128,1024]{1,0:T(8,128)} async-done(((f32[1024,1024]{1,0:T(8,128)}), f32[128,1024]{1,0:T(8,128)}) %reduce-scatter.98.cloned.1.call-update) | async-done | bytes 524304 | tf_op jit(solution)/shard_map/reduce_scatter | solution.py:57
  1747.8 79.3 %reduce-scatter.92.cloned.1.call-done = f32[128,3,256]{2,0,1:T(8,128)} async-done(((f32[1024,3,256]{2,0,1:T(8,128)}), f32[128,3,256]{2,0,1:T(8,128)}) %reduce-scatter.92.cloned.1.call-update) | async-done | bytes 393232 | tf_op jit(solution)/shard_map/reduce_scatter | solution.py:54
  (887 shorter events, 447.7 us)
Async XLA Ops:
  7.2 46.4 %all-gather.22.cloned.1.call-start = ((), (), s32[]{:S(2)}) async-start(), calls=%async_computation.33 | async-start | bytes 1179648 | tf_op jit(solution)/shard_map/all_gather | solution.py:35
  8.8 96.1 %reduce-scatter.34.cloned.1.call-start = ((), (), s32[]{:S(2)}) async-start(), calls=%async_computation.34 | async-start | bytes 2621440 | tf_op jit(solution)/shard_map/reduce_scatter | solution.py:48
  57.0 65.2 %reduce-scatter.40.cloned.1.call-start = ((), (), s32[]{:S(2)}) async-start(), calls=%async_computation.40 | async-start | bytes 2621440 | tf_op jit(solution)/shard_map/reduce_scatter | solution.py:48
  59.2 96.9 %reduce-scatter.46.cloned.1.call-start = ((), (), s32[]{:S(2)}) async-start(), calls=%async_computation.43 | async-start | bytes 2621440 | tf_op jit(solution)/shard_map/reduce_scatter | solution.py:48
  61.4 128.7 %reduce-scatter.52.cloned.1.call-start = ((), (), s32[]{:S(2)}) async-start(), calls=%async_computation.46 | async-start | bytes 2621440 | tf_op jit(solution)/shard_map/reduce_scatter | solution.py:48
  63.6 174.3 %all-gather.24.cloned.1.call-start = ((), (), s32[]{:S(2)}) async-start(), calls=%async_computation.35 | async-start | bytes 1769472 | tf_op jit(solution)/shard_map/all_gather | solution.py:36
  64.5 272.0 %all-gather.36.cloned.1.call-start = ((), (), s32[]{:S(2)}) async-start(), calls=%async_computation.73 | async-start | bytes 1310720 | tf_op jit(solution)/shard_map/all_gather | solution.py:91
  241.2 101.3 %all-gather.34.cloned.1.call-start = ((), (), s32[]{:S(2)}) async-start(), calls=%async_computation.72 | async-start | bytes 1310720 | tf_op jit(solution)/shard_map/all_gather | solution.py:92
  241.9 108.2 %all-gather.40.cloned.1.call-start = ((), (), s32[]{:S(2)}) async-start(), calls=%async_computation.75 | async-start | bytes 1310720 | tf_op jit(solution)/shard_map/all_gather | solution.py:91
  261.2 106.4 %all-gather.38.cloned.1.call-start = ((), (), s32[]{:S(2)}) async-start(), calls=%async_computation.74 | async-start | bytes 1310720 | tf_op jit(solution)/shard_map/all_gather | solution.py:92
  261.8 136.4 %all-gather.44.cloned.1.call-start = ((), (), s32[]{:S(2)}) async-start(), calls=%async_computation.77 | async-start | bytes 1310720 | tf_op jit(solution)/shard_map/all_gather | solution.py:91
  280.0 148.2 %all-gather.42.cloned.1.call-start = ((), (), s32[]{:S(2)}) async-start(), calls=%async_computation.76 | async-start | bytes 1310720 | tf_op jit(solution)/shard_map/all_gather | solution.py:92
  280.5 177.8 %all-gather.32.cloned.1.call-start = ((), (), s32[]{:S(2)}) async-start(), calls=%async_computation.71 | async-start | bytes 1310720 | tf_op jit(solution)/shard_map/all_gather | solution.py:91
  301.1 187.2 %all-gather.30.cloned.1.call-start = ((), (), s32[]{:S(2)}) async-start(), calls=%async_computation.70 | async-start | bytes 1310720 | tf_op jit(solution)/shard_map/all_gather | solution.py:92
  336.4 184.5 %reduce-scatter.42.cloned.1.call-start = ((), (), s32[]{:S(2)}) async-start(), calls=%async_computation.41 | async-start | bytes 2621440 | tf_op jit(solution)/shard_map/reduce_scatter | solution.py:48
  349.9 205.7 %reduce-scatter.48.cloned.1.call-start = ((), (), s32[]{:S(2)}) async-start(), calls=%async_computation.44 | async-start | bytes 2621440 | tf_op jit(solution)/shard_map/reduce_scatter | solution.py:48
  374.8 214.6 %reduce-scatter.54.cloned.1.call-start = ((), (), s32[]{:S(2)}) async-start(), calls=%async_computation.47 | async-start | bytes 2621440 | tf_op jit(solution)/shard_map/reduce_scatter | solution.py:48
  435.4 188.0 %reduce-scatter.36.cloned.1.call-start = ((), (), s32[]{:S(2)}) async-start(), calls=%async_computation.36 | async-start | bytes 2621440 | tf_op jit(solution)/shard_map/reduce_scatter | solution.py:48
  495.5 193.6 %all-gather.26.cloned.1.call-start = ((), (), s32[]{:S(2)}) async-start(), calls=%async_computation.37 | async-start | bytes 2359296 | tf_op jit(solution)/shard_map/all_gather | solution.py:38
  496.2 243.0 %all-gather.28.cloned.1.call-start = ((), (), s32[]{:S(2)}) async-start(), calls=%async_computation.38 | async-start | bytes 2359296 | tf_op jit(solution)/shard_map/all_gather | solution.py:39
  498.3 131.2 %collective-permute-start.51 = (bf16[2,64,1024]{2,1,0:T(8,128)(2,1)}, bf16[2,64,1024]{2,1,0:T(8,128)(2,1)}, u32[]{:S(2)}, u32[]{:S(2)}) collective-permute-start(bf16[2,64,1024]{2,1,0:T(8,128)(2,1)} %get-tuple-element.179), channel_id=1, source_target_pairs={{0,1},{1,2},{2,3},{3,0},{4,5},{5,6},{6,7},{7,4},{8,9},{9,10},{10,1... | collective-permute-start | bytes 786440 | tf_op jit(solution)/shard_map/ppermute | solution.py:16
  627.8 43.9 %collective-permute-start.15 = (bf16[2,64,1024]{2,1,0:T(8,128)(2,1)}, bf16[2,64,1024]{2,1,0:T(8,128)(2,1)}, u32[]{:S(2)}, u32[]{:S(2)}) collective-permute-start(bf16[2,64,1024]{2,1,0:T(8,128)(2,1)} %get-tuple-element.219), channel_id=1, source_target_pairs={{0,1},{1,2},{2,3},{3,0},{4,5},{5,6},{6,7},{7,4},{8,9},{9,10},{10,1... | collective-permute-start | bytes 786440 | tf_op jit(solution)/shard_map/ppermute | solution.py:16
  627.8 45.4 %collective-permute-start.53 = (bf16[2,64,1024]{2,1,0:T(8,128)(2,1)}, bf16[2,64,1024]{2,1,0:T(8,128)(2,1)}, u32[]{:S(2)}, u32[]{:S(2)}) collective-permute-start(bf16[2,64,1024]{2,1,0:T(8,128)(2,1)} %get-tuple-element.179), channel_id=1, source_target_pairs={{0,3},{1,0},{2,1},{3,2},{4,7},{5,4},{6,5},{7,6},{8,11},{9,8},{10,9... | collective-permute-start | bytes 786440 | tf_op jit(solution)/shard_map/ppermute | solution.py:18
  629.5 43.7 %collective-permute-start.52 = (bf16[2,64,1024]{2,1,0:T(8,128)(2,1)}, bf16[2,64,1024]{2,1,0:T(8,128)(2,1)}, u32[]{:S(2)}, u32[]{:S(2)}) collective-permute-start(bf16[2,64,1024]{2,1,0:T(8,128)(2,1)} %collective-permute-done.51), channel_id=1, source_target_pairs={{0,1},{1,2},{2,3},{3,0},{4,5},{5,6},{6,7},{7,4},{8,9},{9,10},{10,1... | collective-permute-start | bytes 786440 | tf_op jit(solution)/shard_map/ppermute | solution.py:16
  629.6 204.4 %reduce-scatter.82.cloned.1.call-start = ((), (), s32[]{:S(2)}) async-start(), calls=%async_computation.61 | async-start | bytes 2621440 | tf_op jit(solution)/shard_map/reduce_scatter | solution.py:48
  671.7 13.1 collective-permute-start.16
  677.3 15.0 collective-permute-start.23
  677.5 16.6 collective-permute-start.9
  677.8 24.1 %collective-permute-start.11 = (bf16[2,64,1024]{2,1,0:T(8,128)(2,1)S(1)}, bf16[2,64,1024]{2,1,0:T(8,128)(2,1)}, u32[]{:S(2)}, u32[]{:S(2)}) collective-permute-start(bf16[2,64,1024]{2,1,0:T(8,128)(2,1)S(1)} %get-tuple-element.218), channel_id=1, source_target_pairs={{0,3},{1,0},{2,1},{3,2},{4,7},{5,4},{6,5},{7,6},{8,11},{9,8},{10,9... | collective-permute-start | bytes 786440 | tf_op jit(solution)/shard_map/ppermute | solution.py:18
  679.7 14.4 collective-permute-start.3
  692.3 14.9 collective-permute-start.5
  748.7 87.2 %reduce-scatter.74.cloned.1.call-start = ((), (), s32[]{:S(2)}) async-start(), calls=%async_computation.57 | async-start | bytes 2621440 | tf_op jit(solution)/shard_map/reduce_scatter | solution.py:48
  774.8 81.5 %reduce-scatter.66.cloned.1.call-start = ((), (), s32[]{:S(2)}) async-start(), calls=%async_computation.53 | async-start | bytes 2621440 | tf_op jit(solution)/shard_map/reduce_scatter | solution.py:48
  801.4 88.9 %reduce-scatter.58.cloned.1.call-start = ((), (), s32[]{:S(2)}) async-start(), calls=%async_computation.49 | async-start | bytes 2621440 | tf_op jit(solution)/shard_map/reduce_scatter | solution.py:48
  801.4 13.7 collective-permute-start.24
  801.5 13.6 collective-permute-start.26
  833.9 219.0 %reduce-scatter.86.cloned.1.call-start = ((), (), s32[]{:S(2)}) async-start(), calls=%async_computation.63 | async-start | bytes 1310720 | tf_op jit(solution)/shard_map/reduce_scatter | solution.py:191
  919.7 133.2 %reduce-scatter.84.cloned.1.call-start = ((), (), s32[]{:S(2)}) async-start(), calls=%async_computation.62 | async-start | bytes 1310720 | tf_op jit(solution)/shard_map/reduce_scatter | solution.py:185
  932.6 129.9 %reduce-scatter.70.cloned.1.call-start = ((), (), s32[]{:S(2)}) async-start(), calls=%async_computation.55 | async-start | bytes 1310720 | tf_op jit(solution)/shard_map/reduce_scatter | solution.py:191
  960.6 101.9 %reduce-scatter.68.cloned.1.call-start = ((), (), s32[]{:S(2)}) async-start(), calls=%async_computation.54 | async-start | bytes 1310720 | tf_op jit(solution)/shard_map/reduce_scatter | solution.py:185
  973.7 97.8 %reduce-scatter.62.cloned.1.call-start = ((), (), s32[]{:S(2)}) async-start(), calls=%async_computation.51 | async-start | bytes 1310720 | tf_op jit(solution)/shard_map/reduce_scatter | solution.py:191
  998.2 89.5 %reduce-scatter.60.cloned.1.call-start = ((), (), s32[]{:S(2)}) async-start(), calls=%async_computation.50 | async-start | bytes 1310720 | tf_op jit(solution)/shard_map/reduce_scatter | solution.py:185
  1011.1 104.8 %reduce-scatter.78.cloned.1.call-start = ((), (), s32[]{:S(2)}) async-start(), calls=%async_computation.59 | async-start | bytes 1310720 | tf_op jit(solution)/shard_map/reduce_scatter | solution.py:191
  1036.0 108.2 %reduce-scatter.76.cloned.1.call-start = ((), (), s32[]{:S(2)}) async-start(), calls=%async_computation.58 | async-start | bytes 1310720 | tf_op jit(solution)/shard_map/reduce_scatter | solution.py:185
  1049.1 128.1 %reduce-scatter.88.cloned.1.call-start = ((), (), s32[]{:S(2)}) async-start(), calls=%async_computation.64 | async-start | bytes 2621440 | tf_op jit(solution)/shard_map/reduce_scatter | solution.py:48
  1057.5 153.9 %reduce-scatter.72.cloned.1.call-start = ((), (), s32[]{:S(2)}) async-start(), calls=%async_computation.56 | async-start | bytes 2621440 | tf_op jit(solution)/shard_map/reduce_scatter | solution.py:48
  1066.4 178.9 %reduce-scatter.64.cloned.1.call-start = ((), (), s32[]{:S(2)}) async-start(), calls=%async_computation.52 | async-start | bytes 2621440 | tf_op jit(solution)/shard_map/reduce_scatter | solution.py:48
  1091.8 187.5 %reduce-scatter.80.cloned.1.call-start = ((), (), s32[]{:S(2)}) async-start(), calls=%async_computation.60 | async-start | bytes 2621440 | tf_op jit(solution)/shard_map/reduce_scatter | solution.py:48
  1148.0 271.6 %reduce-scatter.38.cloned.1.call-start = ((), (), s32[]{:S(2)}) async-start(), calls=%async_computation.39 | async-start | bytes 2621440 | tf_op jit(solution)/shard_map/reduce_scatter | solution.py:48
  1153.5 266.2 %reduce-scatter.44.cloned.1.call-start = ((), (), s32[]{:S(2)}) async-start(), calls=%async_computation.42 | async-start | bytes 2621440 | tf_op jit(solution)/shard_map/reduce_scatter | solution.py:48
  1159.0 260.6 %reduce-scatter.50.cloned.1.call-start = ((), (), s32[]{:S(2)}) async-start(), calls=%async_computation.45 | async-start | bytes 2621440 | tf_op jit(solution)/shard_map/reduce_scatter | solution.py:48
  1164.4 262.0 %reduce-scatter.56.cloned.1.call-start = ((), (), s32[]{:S(2)}) async-start(), calls=%async_computation.48 | async-start | bytes 2621440 | tf_op jit(solution)/shard_map/reduce_scatter | solution.py:48
  1170.0 328.1 %reduce-scatter.90.cloned.1.call-start = ((), (), s32[]{:S(2)}) async-start(), calls=%async_computation.65 | async-start | bytes 2359296 | tf_op jit(solution)/shard_map/reduce_scatter | solution.py:53
  1285.6 19.4 %collective-permute-start.50 = (bf16[2,64,1024]{2,1,0:T(8,128)(2,1)S(1)}, bf16[2,64,1024]{2,1,0:T(8,128)(2,1)S(1)}, u32[]{:S(2)}, u32[]{:S(2)}) collective-permute-start(bf16[2,64,1024]{2,1,0:T(8,128)(2,1)S(1)} %get-tuple-element.176), channel_id=1, source_target_pairs={{0,3},{1,0},{2,1},{3,2},{4,7},{5,4},{6,5},{7,6},{8,11},{9,8},{10,9... | collective-permute-start | bytes 786440 | tf_op jit(solution)/shard_map/ppermute | solution.py:18
  1290.6 21.9 %collective-permute-start.39 = (bf16[2,64,1024]{2,1,0:T(8,128)(2,1)S(1)}, bf16[2,64,1024]{2,1,0:T(8,128)(2,1)S(1)}, u32[]{:S(2)}, u32[]{:S(2)}) collective-permute-start(bf16[2,64,1024]{2,1,0:T(8,128)(2,1)S(1)} %get-tuple-element.175), channel_id=1, source_target_pairs={{0,1},{1,2},{2,3},{3,0},{4,5},{5,6},{6,7},{7,4},{8,9},{9,10},{10,1... | collective-permute-start | bytes 786440 | tf_op jit(solution)/shard_map/ppermute | solution.py:16
  1291.0 36.6 %collective-permute-start.41 = (bf16[2,64,1024]{2,1,0:T(8,128)(2,1)S(1)}, bf16[2,64,1024]{2,1,0:T(8,128)(2,1)S(1)}, u32[]{:S(2)}, u32[]{:S(2)}) collective-permute-start(bf16[2,64,1024]{2,1,0:T(8,128)(2,1)S(1)} %get-tuple-element.175), channel_id=1, source_target_pairs={{0,3},{1,0},{2,1},{3,2},{4,7},{5,4},{6,5},{7,6},{8,11},{9,8},{10,9... | collective-permute-start | bytes 786440 | tf_op jit(solution)/shard_map/ppermute | solution.py:18
  1296.2 25.9 %collective-permute-start.30 = (bf16[2,64,1024]{2,1,0:T(8,128)(2,1)S(1)}, bf16[2,64,1024]{2,1,0:T(8,128)(2,1)S(1)}, u32[]{:S(2)}, u32[]{:S(2)}) collective-permute-start(bf16[2,64,1024]{2,1,0:T(8,128)(2,1)S(1)} %get-tuple-element.174), channel_id=1, source_target_pairs={{0,1},{1,2},{2,3},{3,0},{4,5},{5,6},{6,7},{7,4},{8,9},{9,10},{10,1... | collective-permute-start | bytes 786440 | tf_op jit(solution)/shard_map/ppermute | solution.py:16
  1302.1 22.8 %collective-permute-start.49 = (bf16[2,64,1024]{2,1,0:T(8,128)(2,1)S(1)}, bf16[2,64,1024]{2,1,0:T(8,128)(2,1)S(1)}, u32[]{:S(2)}, u32[]{:S(2)}) collective-permute-start(bf16[2,64,1024]{2,1,0:T(8,128)(2,1)S(1)} %collective-permute-done.48), channel_id=1, source_target_pairs={{0,1},{1,2},{2,3},{3,0},{4,5},{5,6},{6,7},{7,4},{8,9},{9,10},{10,1... | collective-permute-start | bytes 786440 | tf_op jit(solution)/shard_map/ppermute | solution.py:16
  1305.0 25.4 %collective-permute-start.32 = (bf16[2,64,1024]{2,1,0:T(8,128)(2,1)S(1)}, bf16[2,64,1024]{2,1,0:T(8,128)(2,1)S(1)}, u32[]{:S(2)}, u32[]{:S(2)}) collective-permute-start(bf16[2,64,1024]{2,1,0:T(8,128)(2,1)S(1)} %get-tuple-element.174), channel_id=1, source_target_pairs={{0,3},{1,0},{2,1},{3,2},{4,7},{5,4},{6,5},{7,6},{8,11},{9,8},{10,9... | collective-permute-start | bytes 786440 | tf_op jit(solution)/shard_map/ppermute | solution.py:18
  1312.5 15.2 collective-permute-start.40
  1339.0 225.5 %reduce-scatter.94.cloned.1.call-start = ((), (), s32[]{:S(2)}) async-start(), calls=%async_computation.67 | async-start | bytes 1179648 | tf_op jit(solution)/shard_map/reduce_scatter | solution.py:55
  1344.5 311.5 %reduce-scatter.96.cloned.1.call-start = ((), (), s32[]{:S(2)}) async-start(), calls=%async_computation.68 | async-start | bytes 4718592 | tf_op jit(solution)/shard_map/reduce_scatter | solution.py:56
  1353.1 394.7 %reduce-scatter.98.cloned.1.call-start = ((), (), s32[]{:S(2)}) async-start(), calls=%async_computation.69 | async-start | bytes 4718592 | tf_op jit(solution)/shard_map/reduce_scatter | solution.py:57
  1363.7 463.4 %reduce-scatter.92.cloned.1.call-start = ((), (), s32[]{:S(2)}) async-start(), calls=%async_computation.66 | async-start | bytes 3538944 | tf_op jit(solution)/shard_map/reduce_scatter | solution.py:54
  (268 other events, 7719.7 us)
Sparse Core Ops, SparseCore 0:
  10.7 42.8 all-gather.21
  57.1 30.3 reduce-scatter.33
  90.8 31.4 reduce-scatter.39
  124.6 31.4 reduce-scatter.45
  158.6 31.3 reduce-scatter.51
  192.5 45.3 all-gather.23
  241.3 28.3 all-gather.35
  271.8 28.4 all-gather.33
  302.5 34.9 all-gather.39
  339.5 28.0 all-gather.37
  369.7 28.4 all-gather.43
  399.7 28.4 all-gather.41
  429.7 28.4 all-gather.31
  459.7 28.4 all-gather.29
  491.2 29.7 reduce-scatter.41
  524.1 31.4 reduce-scatter.47
  557.9 31.3 reduce-scatter.53
  591.9 31.4 reduce-scatter.35
  625.5 49.2 all-gather.25
  676.7 47.7 all-gather.27
  748.8 27.8 reduce-scatter.81
  779.9 41.5 reduce-scatter.73
  824.0 32.1 reduce-scatter.65
  858.8 31.4 reduce-scatter.57
  919.9 26.8 reduce-scatter.85
  949.0 25.7 reduce-scatter.83
  976.9 25.7 reduce-scatter.69
  1005.8 25.7 reduce-scatter.67
  1033.9 25.7 reduce-scatter.61
  1061.9 25.8 reduce-scatter.59
  1090.1 25.7 reduce-scatter.77
  1118.3 25.7 reduce-scatter.75
  1147.1 30.0 reduce-scatter.87
  1179.9 31.3 reduce-scatter.71
  1213.9 31.4 reduce-scatter.63
  1247.9 31.3 reduce-scatter.79
  1282.3 40.7 reduce-scatter.37
  1325.7 32.0 reduce-scatter.43
  1360.2 32.1 reduce-scatter.49
  1395.0 31.3 reduce-scatter.55
  1429.9 68.0 reduce-scatter.89
  1502.0 62.4 reduce-scatter.93
  1569.0 86.8 reduce-scatter.95
  1660.1 87.6 reduce-scatter.97
  1752.3 74.7 reduce-scatter.91
